TPU v7x, 32 devices: a whole 2x2x4 slice. The times are simulated.
32 devices in a mesh: seq: 4 (over x, core), fsdp: 8 (over z, y).
Axes of the slice: x: 2, y: 2, z: 4, core: 2. Of those that a mesh axis runs over, the one named last changes fastest.
Arguments:
- hidden_in: bfloat16 [8, 1024, 1536], P('fsdp', 'seq'), may hold values from -6 to 6
- positions: int32 [8, 1024], P('fsdp', 'seq'), may hold values from 0 to 5116, as said below
- attn_gain: bfloat16 [1536], P('fsdp'), may hold values from 0.25 to 1.75
- qkv_weight: bfloat16 [1536, 2048], P('fsdp'), may hold values from -0.15625 to 0.15625
- qkv_bias: bfloat16 [2048], P('fsdp'), may hold values from -3 to 3
- out_weight: bfloat16 [1536, 1536], P('fsdp'), may hold values from -1.75 to 1.75
- mlp_gain: bfloat16 [1536], P('fsdp'), may hold values from 0.25 to 1.75
- gate_weight: bfloat16 [8960, 1536], P('fsdp'), may hold values from -0.15625 to 0.15625
- up_weight: bfloat16 [8960, 1536], P('fsdp'), may hold values from -0.15625 to 0.15625
- down_weight: bfloat16 [8960, 1536], P('fsdp'), may hold values from -0.0625 to 0.0625
- cotangent: bfloat16 [8, 1024, 1536], P('fsdp', 'seq'), may hold values from -6 to 6
Outputs:
- hidden_out: bfloat16 [8, 1024, 1536], P('fsdp', 'seq')
- grad_in: float32 [8, 1024, 1536], P('fsdp', 'seq')
- grad_attn_gain: float32 [1536], P('fsdp')
- grad_qkv_weight: float32 [1536, 2048], P('fsdp')
- grad_qkv_bias: float32 [2048], P('fsdp')
- grad_out_weight: float32 [1536, 1536], P('fsdp')
- grad_mlp_gain: float32 [1536], P('fsdp')
- grad_gate_weight: float32 [8960, 1536], P('fsdp')
- grad_up_weight: float32 [8960, 1536], P('fsdp')
- grad_down_weight: float32 [8960, 1536], P('fsdp')
Inputs may be any that keep to these rules, and one draw needn't show every extreme that they name: Along each sequence the positions rise by 1 to 3 from one token to the next; the first lies below 2048.
All inputs are finite; a program needn't handle non-finite values.
Results may differ from a plain program's by a relative error of at most 0.019.
Values may be sent and summed in bfloat16 or wider, within the bound.
A program may use at most 320 MiB of HBM per device.

v0:
```python
import math
import jax
import jax.numpy as jnp
from jax import lax
from jax.sharding import PartitionSpec as P

HEADS = 12
KV_HEADS = 2
HEAD_DIM = 128
norm_eps = 1e-06
rope_base = 1000000.0


def rope_tables(position_row):
    half_dim = HEAD_DIM // 2
    frequency = jnp.exp(
        -(jnp.arange(half_dim, dtype=jnp.float32) * 2.0 / HEAD_DIM) * math.log(rope_base)
    )
    angles = position_row.astype(jnp.float32)[:, None] * frequency[None, :]
    angles = jnp.concatenate([angles, angles], axis=-1)
    return (jnp.cos(angles), jnp.sin(angles))


def rotate(values, cosine, sine):
    half_dim = values.shape[-1] // 2
    turned = jnp.concatenate([-values[..., half_dim:], values[..., :half_dim]], axis=-1)
    return values * cosine[:, None, :] + turned * sine[:, None, :]


def unrotate(grads_rot, cosine, sine):
    half_dim = grads_rot.shape[-1] // 2
    scaled = grads_rot * sine[:, None, :]
    return grads_rot * cosine[:, None, :] + jnp.concatenate(
        [scaled[..., half_dim:], -scaled[..., :half_dim]], axis=-1
    )


def norm_forward(values, gain):
    inverse = lax.rsqrt(jnp.mean(values * values, axis=-1, keepdims=True) + norm_eps)
    unit_rows = values * inverse
    return (unit_rows, inverse, (unit_rows * gain).astype(jnp.bfloat16))


def norm_backward(grad_normed, unit_rows, inverse, gain):
    grad_unit = grad_normed * gain
    grad_values = inverse * (
        grad_unit - unit_rows * jnp.mean(grad_unit * unit_rows, axis=-1, keepdims=True)
    )
    grad_gain = jnp.sum(grad_normed * unit_rows, axis=0)
    return (grad_values, grad_gain)


def masked_scores(queries, keys, block_start, block_rows):
    length = keys.shape[0]
    query_block = lax.dynamic_slice_in_dim(queries, block_start, block_rows, 0)
    scores = jnp.einsum(
        "bhd,ld->hbl", query_block, keys, preferred_element_type=jnp.float32
    ) * HEAD_DIM ** (-0.5)
    row_index = block_start + jnp.arange(block_rows)
    column_index = jnp.arange(length)
    allowed = column_index[None, :] <= row_index[:, None]
    return (query_block, jnp.where(allowed[None], scores, -1e30))


def attend_forward(queries, keys, values):
    length = keys.shape[0]
    block_rows = min(512, length)
    block_count = length // block_rows

    def one_block(block_start):
        query_block, scores = masked_scores(queries, keys, block_start, block_rows)
        row_max = jnp.max(scores, axis=-1, keepdims=True)
        exponent = jnp.exp(scores - row_max)
        row_total = jnp.sum(exponent, axis=-1, keepdims=True)
        probability = (exponent / row_total).astype(jnp.bfloat16)
        result = jnp.einsum("hbl,ld->bhd", probability, values, preferred_element_type=jnp.float32)
        return (result.astype(jnp.bfloat16), (row_max + jnp.log(row_total))[..., 0])

    results, log_totals = lax.map(one_block, jnp.arange(block_count) * block_rows)
    return (results.reshape(length, queries.shape[1], queries.shape[2]), log_totals)


def attend_backward(queries, keys, values, log_totals, grad_out):
    length = keys.shape[0]
    block_rows = min(512, length)
    block_count = length // block_rows
    score_scale = HEAD_DIM ** (-0.5)

    def one_block(running, inputs):
        grad_keys, grad_values = running
        block_start, log_block = inputs
        query_block, scores = masked_scores(queries, keys, block_start, block_rows)
        grad_block = lax.dynamic_slice_in_dim(grad_out, block_start, block_rows, 0)
        probability = jnp.exp(scores - log_block[..., None])
        grad_probs = jnp.einsum(
            "bhd,ld->hbl", grad_block, values, preferred_element_type=jnp.float32
        )
        row_delta = jnp.sum(probability * grad_probs, axis=-1, keepdims=True)
        grad_scores = (probability * (grad_probs - row_delta)).astype(jnp.bfloat16)
        grad_query = (
            jnp.einsum("hbl,ld->bhd", grad_scores, keys, preferred_element_type=jnp.float32)
            * score_scale
        )
        grad_keys = (
            grad_keys
            + jnp.einsum(
                "hbl,bhd->ld", grad_scores, query_block, preferred_element_type=jnp.float32
            )
            * score_scale
        )
        grad_values = grad_values + jnp.einsum(
            "hbl,bhd->ld",
            probability.astype(jnp.bfloat16),
            grad_block,
            preferred_element_type=jnp.float32,
        )
        return ((grad_keys, grad_values), grad_query)

    zero_rows = jnp.zeros((length, keys.shape[1]), jnp.float32)
    (grad_keys, grad_values), grad_query = lax.scan(
        one_block, (zero_rows, zero_rows), (jnp.arange(block_count) * block_rows, log_totals)
    )
    return (grad_query.reshape(queries.shape), grad_keys, grad_values)


def per_device(
    hidden_in,
    positions,
    attn_gain,
    qkv_weight,
    qkv_bias,
    out_weight,
    mlp_gain,
    gate_weight,
    up_weight,
    down_weight,
    cotangent,
):
    groups = lax.axis_size("seq")
    group_heads = HEADS // groups
    repeat = groups // KV_HEADS
    tokens = hidden_in.shape[1]
    width_query = HEADS * HEAD_DIM
    width_key = KV_HEADS * HEAD_DIM
    residual = hidden_in[0].astype(jnp.float32)
    cosine, sine = rope_tables(positions[0])
    gains_one, gains_two, qkv_full, bias_full, out_full = (
        lax.all_gather(attn_gain, "fsdp", axis=0, tiled=True),
        lax.all_gather(mlp_gain, "fsdp", axis=0, tiled=True),
        lax.all_gather(qkv_weight, "fsdp", axis=0, tiled=True),
        lax.all_gather(qkv_bias, "fsdp", axis=0, tiled=True),
        lax.all_gather(out_weight, "fsdp", axis=0, tiled=True),
    )
    gain_one = gains_one.astype(jnp.float32)
    gain_two = gains_two.astype(jnp.float32)
    unit_one, inverse_one, normed_one = norm_forward(residual, gain_one)
    qkv_mixed = jnp.dot(
        normed_one, qkv_full, preferred_element_type=jnp.float32
    ) + bias_full.astype(jnp.float32)
    query_part = qkv_mixed[:, :width_query].reshape(tokens, HEADS, HEAD_DIM)
    key_part = qkv_mixed[:, width_query : width_query + width_key].reshape(
        tokens, KV_HEADS, HEAD_DIM
    )
    value_part = qkv_mixed[:, width_query + width_key :].reshape(tokens, KV_HEADS, HEAD_DIM)
    queries = (
        rotate(query_part, cosine, sine)
        .astype(jnp.bfloat16)
        .reshape(tokens, groups, group_heads * HEAD_DIM)
    )
    keys_rep = jnp.repeat(rotate(key_part, cosine, sine).astype(jnp.bfloat16), repeat, axis=1)
    values_rep = jnp.repeat(value_part.astype(jnp.bfloat16), repeat, axis=1)
    head_queries, head_keys, head_values = (
        lax.all_to_all(queries, "seq", split_axis=1, concat_axis=0, tiled=True),
        lax.all_to_all(keys_rep, "seq", split_axis=1, concat_axis=0, tiled=True),
        lax.all_to_all(values_rep, "seq", split_axis=1, concat_axis=0, tiled=True),
    )
    head_queries = head_queries.reshape(-1, group_heads, HEAD_DIM)
    head_keys = head_keys.reshape(-1, HEAD_DIM)
    head_values = head_values.reshape(-1, HEAD_DIM)
    attended, log_totals = attend_forward(head_queries, head_keys, head_values)
    returned = lax.all_to_all(
        attended.reshape(-1, 1, group_heads * HEAD_DIM),
        "seq",
        split_axis=0,
        concat_axis=1,
        tiled=True,
    )
    attn_rows = returned.reshape(tokens, width_query)
    residual_two = residual + jnp.dot(attn_rows, out_full, preferred_element_type=jnp.float32)
    unit_two, inverse_two, normed_two = norm_forward(residual_two, gain_two)
    grad_output = cotangent[0].astype(jnp.float32)
    grad_mlp = grad_output.astype(jnp.bfloat16)
    all_rows = lax.all_gather(normed_two, "fsdp", axis=0, tiled=True)
    gate_pre = jnp.einsum("td,fd->tf", all_rows, gate_weight, preferred_element_type=jnp.float32)
    up_pre = jnp.einsum("td,fd->tf", all_rows, up_weight, preferred_element_type=jnp.float32)
    sigmoid_gate = jax.nn.sigmoid(gate_pre)
    activated = gate_pre * sigmoid_gate
    hidden = (activated * up_pre).astype(jnp.bfloat16)
    partial_out = jnp.dot(hidden, down_weight, preferred_element_type=jnp.float32)
    mlp_out = lax.psum_scatter(
        partial_out.astype(jnp.bfloat16), "fsdp", scatter_dimension=0, tiled=True
    ).astype(jnp.float32)
    all_grads = lax.all_gather(grad_mlp, "fsdp", axis=0, tiled=True)
    grad_hidden = jnp.einsum(
        "tm,fm->tf", all_grads, down_weight, preferred_element_type=jnp.float32
    )
    grad_gate = (
        grad_hidden * up_pre * sigmoid_gate * (1.0 + gate_pre * (1.0 - sigmoid_gate))
    ).astype(jnp.bfloat16)
    grad_up = (grad_hidden * activated).astype(jnp.bfloat16)
    partial_back = jnp.dot(grad_gate, gate_weight, preferred_element_type=jnp.float32) + jnp.dot(
        grad_up, up_weight, preferred_element_type=jnp.float32
    )
    grad_normed_two = lax.psum_scatter(partial_back, "fsdp", scatter_dimension=0, tiled=True)
    shard_gate = jnp.einsum("tf,td->fd", grad_gate, all_rows, preferred_element_type=jnp.float32)
    shard_up = jnp.einsum("tf,td->fd", grad_up, all_rows, preferred_element_type=jnp.float32)
    shard_down = jnp.einsum("tf,td->fd", hidden, all_grads, preferred_element_type=jnp.float32)
    hidden_out = (residual_two + mlp_out).astype(jnp.bfloat16)
    grad_norm_two, term_gain_two = norm_backward(grad_normed_two, unit_two, inverse_two, gain_two)
    grad_residual_two = grad_output + grad_norm_two
    grad_proj = grad_residual_two.astype(jnp.bfloat16)
    grad_attn_rows = jnp.einsum(
        "td,ed->te", grad_proj, out_full, preferred_element_type=jnp.float32
    ).astype(jnp.bfloat16)
    term_out = jnp.einsum("te,td->ed", attn_rows, grad_proj, preferred_element_type=jnp.float32)
    grad_heads = lax.all_to_all(
        grad_attn_rows.reshape(tokens, groups, group_heads * HEAD_DIM),
        "seq",
        split_axis=1,
        concat_axis=0,
        tiled=True,
    )
    grad_query, grad_keys, grad_values = attend_backward(
        head_queries,
        head_keys,
        head_values,
        log_totals,
        grad_heads.reshape(-1, group_heads, HEAD_DIM),
    )
    back_query, back_keys, back_values = (
        lax.all_to_all(
            grad_query.astype(jnp.bfloat16).reshape(-1, 1, group_heads * HEAD_DIM),
            "seq",
            split_axis=0,
            concat_axis=1,
            tiled=True,
        ),
        lax.all_to_all(
            grad_keys.astype(jnp.bfloat16)[:, None, :],
            "seq",
            split_axis=0,
            concat_axis=1,
            tiled=True,
        ),
        lax.all_to_all(
            grad_values.astype(jnp.bfloat16)[:, None, :],
            "seq",
            split_axis=0,
            concat_axis=1,
            tiled=True,
        ),
    )
    grad_query_rows = unrotate(
        back_query.reshape(tokens, HEADS, HEAD_DIM).astype(jnp.float32), cosine, sine
    )
    grad_key_rows = unrotate(
        jnp.sum(back_keys.astype(jnp.float32).reshape(tokens, KV_HEADS, repeat, HEAD_DIM), axis=2),
        cosine,
        sine,
    )
    grad_value_rows = jnp.sum(
        back_values.astype(jnp.float32).reshape(tokens, KV_HEADS, repeat, HEAD_DIM), axis=2
    )
    grad_mixed = jnp.concatenate(
        [
            grad_query_rows.reshape(tokens, width_query),
            grad_key_rows.reshape(tokens, width_key),
            grad_value_rows.reshape(tokens, width_key),
        ],
        axis=1,
    ).astype(jnp.bfloat16)
    term_qkv = jnp.einsum("td,tc->dc", normed_one, grad_mixed, preferred_element_type=jnp.float32)
    term_bias = jnp.sum(grad_mixed.astype(jnp.float32), axis=0)
    grad_normed_one = jnp.einsum(
        "tc,dc->td", grad_mixed, qkv_full, preferred_element_type=jnp.float32
    )
    grad_norm_one, term_gain_one = norm_backward(grad_normed_one, unit_one, inverse_one, gain_one)
    grad_rows = grad_residual_two + grad_norm_one
    shard_gain_one, shard_qkv, shard_bias, shard_out, shard_gain_two = (
        lax.psum_scatter(
            term_gain_one.astype(jnp.bfloat16), "fsdp", scatter_dimension=0, tiled=True
        ).astype(jnp.float32),
        lax.psum_scatter(
            term_qkv.astype(jnp.bfloat16), "fsdp", scatter_dimension=0, tiled=True
        ).astype(jnp.float32),
        lax.psum_scatter(
            term_bias.astype(jnp.bfloat16), "fsdp", scatter_dimension=0, tiled=True
        ).astype(jnp.float32),
        lax.psum_scatter(
            term_out.astype(jnp.bfloat16), "fsdp", scatter_dimension=0, tiled=True
        ).astype(jnp.float32),
        lax.psum_scatter(
            term_gain_two.astype(jnp.bfloat16), "fsdp", scatter_dimension=0, tiled=True
        ).astype(jnp.float32),
    )
    totals = (
        lax.psum(shard_gain_one.astype(jnp.bfloat16), "seq").astype(jnp.float32),
        lax.psum(shard_qkv.astype(jnp.bfloat16), "seq").astype(jnp.float32),
        lax.psum(shard_bias.astype(jnp.bfloat16), "seq").astype(jnp.float32),
        lax.psum(shard_out.astype(jnp.bfloat16), "seq").astype(jnp.float32),
        lax.psum(shard_gain_two.astype(jnp.bfloat16), "seq").astype(jnp.float32),
        lax.psum(shard_gate.astype(jnp.bfloat16), "seq").astype(jnp.float32),
        lax.psum(shard_up.astype(jnp.bfloat16), "seq").astype(jnp.float32),
        lax.psum(shard_down.astype(jnp.bfloat16), "seq").astype(jnp.float32),
    )
    return (
        hidden_out[None],
        grad_rows[None],
        totals[0],
        totals[1],
        totals[2],
        totals[3],
        totals[4],
        totals[5],
        totals[6],
        totals[7],
    )


def solution(mesh):
    placed = (
        P("fsdp", "seq", None),
        P("fsdp", "seq"),
        P("fsdp"),
        P("fsdp", None),
        P("fsdp"),
        P("fsdp", None),
        P("fsdp"),
        P("fsdp", None),
        P("fsdp", None),
        P("fsdp", None),
        P("fsdp", "seq", None),
    )
    return jax.shard_map(
        per_device,
        mesh=mesh,
        in_specs=placed,
        out_specs=(
            P("fsdp", "seq", None),
            P("fsdp", "seq", None),
            P("fsdp"),
            P("fsdp", None),
            P("fsdp"),
            P("fsdp", None),
            P("fsdp"),
            P("fsdp", None),
            P("fsdp", None),
            P("fsdp", None),
        ),
        check_vma=False,
    )
```

profile of v0, /device:TPU:0, one launch (start us, length us, event | category | flops | bytes accessed | tf_op | source)
XLA Modules:
  0.0 1280.1 jit_solution(13989524856095700904)
XLA Ops:
  12.4 23.9 %all-reduce.6 = (bf16[1536]{0:T(1024)(128)(2,1)S(1)}, bf16[1536]{0:T(1024)(128)(2,1)S(1)}) all-reduce(bf16[1536]{0:T(1024)(128)(2,1)S(1)} %dynamic-update-slice, bf16[1536]{0:T(1024)(128)(2,1)S(1)} %dynamic-update-slice.1), channel_id=1, replica_groups=mesh['seq'=4,'fsdp'=8] {'fsdp'}, use_global_device_ids=true, to_apply=%add | all-reduce | flops 3072 | bytes 12288
  38.4 16.5 %all-gather.1 = bf16[8,1,256]{2,1,0:T(2,128)(2,1)S(1)} all-gather(bf16[1,1,256]{2,1,0:T(2,128)(2,1)S(1)} %reshape.306), channel_id=1, replica_groups=mesh['seq'=4,'fsdp'=8] {'fsdp'}, dimensions={0}, use_global_device_ids=true | all-gather | bytes 4608 | tf_op jit(solution)/shard_map/all_gather | solution.py:151
  60.3 52.2 %all-gather.7.cloned.1.call-done = bf16[1536,2048]{1,0:T(8,128)(2,1)} async-done(((bf16[192,2048]{1,0:T(8,128)(2,1)}), bf16[1536,2048]{1,0:T(8,128)(2,1)}) %all-gather.7.cloned.1.call-update) | async-done | bytes 6291472 | tf_op jit(solution)/shard_map/all_gather | solution.py:150
  112.5 4.9 convolution_add_fusion.2
  120.0 3.2 copy.120
  126.3 4.0 all-to-all-start.1
  136.4 4.2 all-to-all-start
  142.2 10.1 all-to-all-done
  154.0 4.5 all-to-all-start.2
  165.9 23.9 %while.27 = (s32[]{:T(128)}, bf16[2,512,3,128]{3,1,2,0:T(8,128)(2,1)}, f32[2,3,512]{2,1,0:T(4,128)S(1)}, s32[2]{0:T(128)S(1)}, bf16[1024,3,128]{2,0,1:T(8,128)(2...) while((s32[]{:T(128)}, ...), condition=%wide.region_4.5_spmd, body=%wide.region_1.4_spmd.sunk | while | flops 824900608 | bytes 22342304 | solution.py:79
  169.5 2.7 bitcast_reduce_fusion.2
  174.0 3.8 fusion.127
  181.4 2.7 bitcast_reduce_fusion.2
  186.0 3.8 fusion.127
  189.8 2.8 copy.121
  192.6 5.6 reshape.319
  198.7 7.3 reduce.2
  207.9 4.2 all-to-all-start.3
  212.2 11.7 all-to-all-done.3
  223.8 3.7 reshape.325
  232.3 4.3 multiply_reduce_fusion.2
  239.6 95.6 %all-gather.11.cloned.1.call-done = bf16[2048,1536]{1,0:T(8,128)(2,1)} async-done(((bf16[256,1536]{1,0:T(8,128)(2,1)}), bf16[2048,1536]{1,0:T(8,128)(2,1)}) %all-gather.11.cloned.1.call-update) | async-done | bytes 6291472 | tf_op jit(solution)/shard_map/all_gather | solution.py:193
  335.2 13.4 %fusion.80 = f32[2048,1120]{0,1:T(8,128)} fusion(bf16[2048,1536]{1,0:T(8,128)(2,1)} %all-gather.11.cloned.1.call-done, bf16[1120,1536]{1,0:T(8,128)(2,1)} %param.22), kind=kOutput, calls=%fused_computation.140 | convolution fusion | flops 7046430720 | bytes 18907136 | tf_op jit(solution)/shard_map/td,fd->tf/dot_general | solution.py:194
  348.6 9.6 fusion.81
  358.2 76.3 %all-gather.13.cloned.1.call-done = bf16[1,2048,1536]{2,1,0:T(8,128)(2,1)} async-done(((bf16[1,256,1536]{2,1,0:T(8,128)(2,1)}), bf16[1,2048,1536]{2,1,0:T(8,128)(2,1)}) %all-gather.13.cloned.1.call-update) | async-done | bytes 6291472 | tf_op jit(solution)/shard_map/all_gather | solution.py:203
  434.5 18.3 %multiply_convert_fusion = (bf16[2048,1120]{0,1:T(8,128)(2,1)}, bf16[2048,1120]{0,1:T(8,128)(2,1)}, bf16[2048,1120]{0,1:T(8,128)(2,1)}) fusion(f32[2048,1120]{0,1:T(8,128)} %fusion.80, f32[2048,1120]{0,1:T(8,128)} %fusion.81, bf16[1120,1536]{1,0:T(8,128)(2,1)S(1)} %copy-done, bf16[1,2048,1536]{2,1,0:T(8,128)(2,1)} %all-gather.13.cloned.1.call-done), kind=kOutput, calls=%fused_computation.56 | convolution fusion | flops 7080837120 | bytes 41844736 | tf_op jit(solution)/shard_map/tm,fm->tf/dot_general | solution.py:204
  452.8 13.0 %fusion.82 = f32[2048,1536]{1,0:T(8,128)} fusion(bf16[2048,1120]{0,1:T(8,128)(2,1)} %get-tuple-element.264, bf16[1120,1536]{1,0:T(8,128)(2,1)S(1)} %copy-done.31), kind=kOutput, calls=%fused_computation.142 | convolution fusion | flops 7046430720 | bytes 20611072 | tf_op jit(solution)/shard_map/dot_general | solution.py:211
  465.9 14.2 %convolution_add_fusion = f32[2048,1536]{1,0:T(8,128)} fusion(f32[2048,1536]{1,0:T(8,128)} %fusion.82, bf16[2048,1120]{0,1:T(8,128)(2,1)S(1)} %copy-done.34, bf16[1120,1536]{1,0:T(8,128)(2,1)S(1)} %copy-done.33), kind=kOutput, calls=%fused_computation.61 | convolution fusion | flops 7049576448 | bytes 33193984 | tf_op jit(solution)/shard_map/dot_general | solution.py:211
  480.1 12.4 convolution_convert_fusion
  492.6 193.1 %reduce-scatter.7.cloned.1.call-done = f32[256,1536]{1,0:T(8,128)} async-done(((f32[2048,1536]{1,0:T(8,128)}), f32[256,1536]{1,0:T(8,128)}) %reduce-scatter.7.cloned.1.call-update) | async-done | bytes 1572880 | tf_op jit(solution)/shard_map/reduce_scatter | solution.py:214
  688.2 118.6 %reduce-scatter.5.cloned.1.call-done = bf16[256,1536]{1,0:T(8,128)(2,1)} async-done(((bf16[2048,1536]{1,0:T(8,128)(2,1)}), bf16[256,1536]{1,0:T(8,128)(2,1)}) %reduce-scatter.5.cloned.1.call-update) | async-done | bytes 786448 | tf_op jit(solution)/shard_map/reduce_scatter | solution.py:200
  806.8 3.2 convert_add_fusion
  810.1 4.3 convolution_convert_fusion.6
  815.5 3.5 all-to-all-start.4
  819.1 3.6 convolution_convert_fusion.5
  822.7 7.9 all-to-all-done.4
  831.8 46.7 %while.28 = (s32[]{:T(128)}, f32[1024,128]{1,0:T(8,128)}, f32[1024,128]{1,0:T(8,128)}, bf16[2,512,3,128]{3,1,2,0:T(8,128)(2,1)}, s32[2]{0:T(128)S(1)}, /*index=5...) while((s32[]{:T(128)}, f32[1024,128]{1,0:T(8,128)}, ...), condition=%wide.region_11.12_spmd.clone, body=%wide.region_9.11_spmd.clone.sunk | while | flops 2038234112 | bytes 90227544 | solution.py:120
  837.6 4.3 fusion.137
  843.8 2.7 fusion.141
  846.5 2.9 fusion.139
  849.4 6.0 fusion.140
  860.7 4.3 fusion.137
  866.9 2.7 fusion.141
  869.6 3.0 fusion.139
  872.6 6.0 fusion.140
  881.5 3.4 all-to-all-start.6
  886.5 4.4 all-to-all-done.6
  890.9 3.6 all-to-all-start.7
  897.1 5.4 reduce.5
  904.5 3.5 all-to-all-start.5
  909.9 9.7 all-to-all-done.5
  925.0 4.7 convolution_convert_fusion.1
  929.8 12.4 convolution_convert_fusion.3
  942.2 12.1 convolution_convert_fusion.4
  954.4 8.8 convolution_convert_fusion.2
  963.2 83.0 %reduce-scatter.9.cloned.1.call-done = bf16[192,2048]{1,0:T(8,128)(2,1)} async-done(((bf16[1536,2048]{1,0:T(8,128)(2,1)}), bf16[192,2048]{1,0:T(8,128)(2,1)}) %reduce-scatter.9.cloned.1.call-update) | async-done | bytes 786448 | tf_op jit(solution)/shard_map/reduce_scatter | solution.py:293
  1047.8 6.1 fusion.60
  1053.9 35.3 %all-reduce.5 = (bf16[1536]{0:T(1024)(128)(2,1)S(1)}, bf16[2048]{0:T(1024)(128)(2,1)S(1)}, bf16[1536]{0:T(1024)(128)(2,1)S(1)}) all-reduce(bf16[1536]{0:T(1024)(128)(2,1)S(1)} %get-tuple-element.210, bf16[2048]{0:T(1024)(128)(2,1)S(1)} %fusion.75, bf16[1536]{0:T(1024)(128)(2,1)S(1)} %copy-done.29), channel_id=5, replica_groups=mesh['seq'=4,'fsdp'=8] {'fsdp'}, use_global_device_ids=true, to_apply=%region_16.17.clone | all-reduce | flops 5120 | bytes 20480
  1089.4 6.5 all-reduce.7
  1097.7 3.0 fusion.59
  1100.7 156.5 %all-reduce.11.cloned.1.call-done = (bf16[192,2048]{1,0:T(8,128)(2,1)}, bf16[192,1536]{1,0:T(8,128)(2,1)}, bf16[1120,1536]{1,0:T(8,128)(2,1)}, bf16[1120,1536]{1,0:T(8,128)(2,1)}, bf16[1120,1536]{1,0:T(8,128)(2,1)}) async-done(((bf16[192,2048]{1,0:T(8,128)(2,1)}, bf16[192,1536]{1,0:T(8,128)(2,1)}, bf16[1120,1536]{1,0:T(8,128)(2,1)}, bf16[1120,1536]{1,0:T(8,128)(2,1)}, bf16[1120,1536]{1,0:T(8,128)(2,1)}), ...) | async-done | bytes 11698192 | tf_op jit(solution)/shard_map/psum | solution.py:308
  1257.2 6.0 convert_element_type.265
  1263.1 3.9 convert_element_type.267
  1267.0 3.8 convert_element_type.269
  (220 shorter events, 88.5 us)
Async XLA Ops:
  7.2 427.3 %copy-start = (bf16[1120,1536]{1,0:T(8,128)(2,1)S(1)}, bf16[1120,1536]{1,0:T(8,128)(2,1)}, u32[]{:S(2)}) copy-start(bf16[1120,1536]{1,0:T(8,128)(2,1)} %param.24) | copy-start | bytes 10321924
  7.2 105.3 %all-gather.7.cloned.1.call-start = ((), (), s32[]{:S(2)}) async-start(), calls=%async_computation.12 | async-start | bytes 7077888 | tf_op jit(solution)/shard_map/all_gather | solution.py:150
  7.9 224.3 %all-gather.9.cloned.1.call-start = ((), (), s32[]{:S(2)}) async-start(), calls=%async_computation.13 | async-start | bytes 5308416 | tf_op jit(solution)/shard_map/all_gather | solution.py:152
  36.4 81.1 %copy-start.25 = (f32[1536]{0:T(1024)}, f32[1536]{0:T(1024)S(1)}, u32[]{:S(2)}) copy-start(f32[1536]{0:T(1024)S(1)} %convert_element_type.218) | copy-start | bytes 18436
  37.8 79.7 %copy-start.27 = (f32[256]{0:T(256)}, f32[256]{0:T(256)S(1)}, u32[]{:S(2)}) copy-start(f32[256]{0:T(256)S(1)} %add_rsqrt_fusion.1) | copy-start | bytes 3076
  117.4 1.3 copy-start.16
  126.3 10.1 all-to-all-start.1
  130.3 2.7 copy-start.20
  130.3 2.8 copy-start.9
  136.4 15.9 %all-to-all-start = ((bf16[256,4,384]{0,2,1:T(8,128)(2,1)}), bf16[256,4,384]{0,2,1:T(8,128)(2,1)}, u32[]{:S(2)}, u32[]{:S(2)}) async-start(bf16[256,4,384]{0,2,1:T(8,128)(2,1)} %fusion.63), calls=%async_computation | async-start | bytes 1572864 | tf_op jit(solution)/shard_map/all_to_all | solution.py:173
  154.0 12.0 all-to-all-start.2
  207.9 15.9 %all-to-all-start.3 = ((bf16[4,2,49152]{2,1,0:T(2,128)(2,1)}), bf16[4,2,49152]{2,1,0:T(2,128)(2,1)}, u32[]{:S(2)}, u32[]{:S(2)}) async-start(bf16[4,2,49152]{2,1,0:T(2,128)(2,1)} %reshape.324), calls=%async_computation.3 | async-start | bytes 1572864 | tf_op jit(solution)/shard_map/all_to_all | solution.py:181
  212.1 123.1 %all-gather.11.cloned.1.call-start = ((), (), s32[]{:S(2)}) async-start(), calls=%async_computation.14 | async-start | bytes 7077888 | tf_op jit(solution)/shard_map/all_gather | solution.py:193
  236.5 1.1 copy-start.5
  238.8 195.7 %all-gather.13.cloned.1.call-start = ((), (), s32[]{:S(2)}) async-start(), calls=%async_computation.19 | async-start | bytes 7077888 | tf_op jit(solution)/shard_map/all_gather | solution.py:203
  239.4 446.4 %reduce-scatter.7.cloned.1.call-start = ((), (), s32[]{:S(2)}) async-start(), calls=%async_computation.16 | async-start | bytes 14155776 | tf_op jit(solution)/shard_map/reduce_scatter | solution.py:214
  335.2 13.4 %copy-start.30 = (bf16[2048,1536]{1,0:T(8,128)(2,1)S(1)}, bf16[2048,1536]{1,0:T(8,128)(2,1)}, u32[]{:S(2)}) copy-start(bf16[2048,1536]{1,0:T(8,128)(2,1)} %all-gather.11.cloned.1.call-done) | copy-start | bytes 18874372
  335.2 13.4 %copy-start.32 = (bf16[1120,1536]{1,0:T(8,128)(2,1)S(1)}, bf16[1120,1536]{1,0:T(8,128)(2,1)}, u32[]{:S(2)}) copy-start(bf16[1120,1536]{1,0:T(8,128)(2,1)} %param.23) | copy-start | bytes 10321924
  434.5 18.3 %copy-start.31 = (bf16[1120,1536]{1,0:T(8,128)(2,1)S(1)}, bf16[1120,1536]{1,0:T(8,128)(2,1)}, u32[]{:S(2)}) copy-start(bf16[1120,1536]{1,0:T(8,128)(2,1)} %param.22) | copy-start | bytes 10321924
  452.8 13.0 %copy-start.33 = (bf16[1120,1536]{1,0:T(8,128)(2,1)S(1)}, bf16[1120,1536]{1,0:T(8,128)(2,1)}, u32[]{:S(2)}) copy-start(bf16[1120,1536]{1,0:T(8,128)(2,1)} %param.23) | copy-start | bytes 10321924
  452.8 13.0 %copy-start.34 = (bf16[2048,1120]{0,1:T(8,128)(2,1)S(1)}, bf16[2048,1120]{0,1:T(8,128)(2,1)}, u32[]{:S(2)}) copy-start(bf16[2048,1120]{0,1:T(8,128)(2,1)} %get-tuple-element.263) | copy-start | bytes 13762564
  480.1 326.7 %reduce-scatter.5.cloned.1.call-start = ((), (), s32[]{:S(2)}) async-start(), calls=%async_computation.15 | async-start | bytes 7077888 | tf_op jit(solution)/shard_map/reduce_scatter | solution.py:200
  492.6 193.2 %copy-start.6 = (f32[256,1536]{1,0:T(8,128)S(1)}, f32[256,1536]{1,0:T(8,128)}, u32[]{:S(2)}) copy-start(f32[256,1536]{1,0:T(8,128)} %copy-done.5) | copy-start | bytes 4718596
  810.0 9.1 copy-start.10
  814.4 4.8 copy-start.7
  815.5 15.1 %all-to-all-start.4 = ((bf16[256,4,384]{0,2,1:T(8,128)(2,1)}), bf16[256,4,384]{0,2,1:T(8,128)(2,1)S(1)}, u32[]{:S(2)}, u32[]{:S(2)}) async-start(bf16[256,4,384]{0,2,1:T(8,128)(2,1)} %bitcast.275), calls=%async_computation.6 | async-start | bytes 1572864 | tf_op jit(solution)/shard_map/all_to_all | solution.py:226
  819.0 144.1 %reduce-scatter.11.cloned.1.call-start = ((), (), s32[]{:S(2)}) async-start(), calls=%async_computation.18 | async-start | bytes 5308416 | tf_op jit(solution)/shard_map/reduce_scatter | solution.py:299
  832.3 5.4 copy-start.12
  836.6 5.3 copy-start.2
  837.6 4.3 copy-start.3
  846.5 2.9 copy-start.4
  849.4 6.0 copy-start.13
  855.4 5.3 copy-start.12
  859.7 5.3 copy-start.2
  860.6 4.3 copy-start.3
  869.6 3.0 copy-start.4
  872.6 6.0 copy-start.13
  881.5 9.4 all-to-all-start.6
  890.9 13.6 %all-to-all-start.7 = ((bf16[4,2,16384]{2,1,0:T(2,128)(2,1)}), bf16[4,2,16384]{2,1,0:T(2,128)(2,1)S(1)}, u32[]{:S(2)}, u32[]{:S(2)}) async-start(bf16[4,2,16384]{2,1,0:T(2,128)(2,1)} %reshape.326), calls=%async_computation.9 | async-start | bytes 524288 | tf_op jit(solution)/shard_map/all_to_all | solution.py:255
  902.5 5.5 copy-start.17
  902.6 5.6 copy-start.18
  904.4 3.8 copy-start.22
  904.5 15.1 %all-to-all-start.5 = ((bf16[4,2,49152]{2,1,0:T(2,128)(2,1)}), bf16[4,2,49152]{2,1,0:T(2,128)(2,1)S(1)}, u32[]{:S(2)}, u32[]{:S(2)}) async-start(bf16[4,2,49152]{2,1,0:T(2,128)(2,1)} %reshape.330), calls=%async_computation.7 | async-start | bytes 1572864 | tf_op jit(solution)/shard_map/all_to_all | solution.py:241
  908.0 138.2 %reduce-scatter.9.cloned.1.call-start = ((), (), s32[]{:S(2)}) async-start(), calls=%async_computation.17 | async-start | bytes 7077888 | tf_op jit(solution)/shard_map/reduce_scatter | solution.py:293
  920.3 3.3 copy-start.19
  923.7 0.9 copy-start.21
  923.9 1.2 copy-start.8
  923.9 1.1 copy-start.26
  923.9 1.1 copy-start.28
  929.7 327.4 %all-reduce.11.cloned.1.call-start = ((), (), s32[]{:S(2)}) async-start(), calls=%async_computation.20 | async-start | bytes 23396352 | tf_op jit(solution)/shard_map/psum | solution.py:308
  929.8 24.6 %slice-start = ((s8[6291456]{0:T(1024)(128)(4,1)}), s8[4194304]{0:T(1024)(128)(4,1)S(1)}, s32[]{:S(2)}) async-start(s8[6291456]{0:T(1024)(128)(4,1)} %bitcast.290), calls=%async_computation.21 | async-start | bytes 8388608
  929.8 24.6 %slice-start.2 = ((s8[4587520]{0:T(1024)(128)(4,1)}), s8[4194304]{0:T(1024)(128)(4,1)S(1)}, s32[]{:S(2)}) async-start(s8[4587520]{0:T(1024)(128)(4,1)} %bitcast.292), calls=%async_computation.23 | async-start | bytes 8388608
  942.2 12.2 slice-start.1
  942.2 12.2 slice-start.3
  1047.8 6.1 copy-start.29
  1047.8 49.9 %copy-start.11 = (f32[256,1536]{1,0:T(8,128)S(1)}, f32[256,1536]{1,0:T(8,128)}, u32[]{:S(2)}) copy-start(f32[256,1536]{1,0:T(8,128)} %copy-done.10) | copy-start | bytes 4718596
  1257.2 6.0 copy-start.15
  1263.1 3.9 copy-start.14
  1267.0 3.9 copy-start.23
  1267.0 5.2 copy-start.24
  1267.0 6.3 copy-start.1
Sparse Core Ops, SparseCore 0:
  10.2 102.2 all-gather.6
  114.7 78.0 all-gather.8
  238.9 96.2 all-gather.10
  337.2 97.2 all-gather.12
  480.2 205.4 reduce-scatter.6
  689.7 117.0 reduce-scatter.4
  824.1 95.0 reduce-scatter.10
  929.8 116.2 reduce-scatter.8
  1049.7 207.3 all-reduce.10
where the time goes:
time: 1290 us; the launch traced here: 1280 us
  waiting for transfers between devices  823 us (64%)
  matrix products  191 us (15%)
  blocking collectives  82.2 us (6%)
  other arithmetic  66.4 us (5%)
  local copies, waits for them, and re-layouts  61.1 us (5%)
  starting transfers between devices  31.4 us (2%)
  between operations  16.8 us (1%)
    reduce_scatter x1, waiting for transfers between devices, per_device(): lax.psum_scatter(partial_back, 'fsdp', scatter_dimension=0, tiled=True)  193 us
    psum x1, waiting for transfers between devices, per_device(): lax.psum(shard_qkv.astype(jnp.bfloat16), 'seq').astype(jnp.float32)  156 us
    reduce_scatter x1, waiting for transfers between devices, per_device(): lax.psum_scatter(partial_out.astype(jnp.bfloat16), 'fsdp', scatter_dimens...  119 us
    all_gather x1, waiting for transfers between devices, per_device(): all_rows = lax.all_gather(normed_two, 'fsdp', axis=0, tiled=True)  95.6 us
    reduce_scatter x1, waiting for transfers between devices, per_device(): lax.psum_scatter(term_qkv.astype(jnp.bfloat16), 'fsdp', scatter_dimension...  83 us
    all_gather x1, waiting for transfers between devices, per_device(): all_grads = lax.all_gather(grad_mlp, 'fsdp', axis=0, tiled=True)  76.3 us
    unnamed x2, blocking collectives  59.2 us
    all_gather x1, waiting for transfers between devices, per_device(): lax.all_gather(qkv_weight, 'fsdp', axis=0, tiled=True)  52.2 us
  transfers between devices with their start and end apart: 17, of which 13 were waited for; matrix products, arithmetic and copies ran while one was open for 19% of the time, Pallas kernels for 0%

commit v1 on v0

--- a/solution.py
+++ b/solution.py
@@ -200,7 +200,12 @@
     mlp_out = lax.psum_scatter(
         partial_out.astype(jnp.bfloat16), "fsdp", scatter_dimension=0, tiled=True
     ).astype(jnp.float32)
-    all_grads = lax.all_gather(grad_mlp, "fsdp", axis=0, tiled=True)
+    ring = [grad_mlp]
+    for hop in range(7):
+        ring.append(lax.ppermute(ring[-1], "fsdp", [(dev, (dev + 1) % 8) for dev in range(8)]))
+    all_grads = jnp.roll(
+        jnp.concatenate(ring[::-1], axis=0), (lax.axis_index("fsdp") + 1) * ring[0].shape[0], axis=0
+    )
     grad_hidden = jnp.einsum(
         "tm,fm->tf", all_grads, down_weight, preferred_element_type=jnp.float32
     )

time: 1290 us -> 1340 us (1.039)
  waiting for transfers between devices: 823 us -> 851 us
  local copies, waits for them, and re-layouts: 61.1 us -> 86.5 us
    ppermute x0 -> x7, waiting for transfers between devices: none -> 201 us  [per_device(): lax.ppermute(ring[-1], 'fsdp', [(dev, (dev + 1) % 8) for dev in range(8)])]
    all_gather x1, waiting for transfers between devices: 95.6 us -> 0.01 us  [per_device(): all_rows = lax.all_gather(normed_two, 'fsdp', axis=0, tiled=True)]
    all_gather x1 -> x0, waiting for transfers between devices: 76.3 us -> none  [per_device(): all_grads = lax.all_gather(grad_mlp, 'fsdp', axis=0, tiled=True)]
    unnamed x87 -> x116, local copies, waits for them, and re-layouts: 20 us -> 44.3 us
  transfers between devices with their start and end apart: 17 -> 23, of which waited for: 13 -> 18; matrix products, arithmetic and copies ran while one was open for 19% -> 18% of each run, Pallas kernels for 0% -> 0%
where the time goes in v1:
time: 1340 us
  waiting for transfers between devices  851 us (64%)
  matrix products  192 us (14%)
  local copies, waits for them, and re-layouts  86.5 us (6%)
  blocking collectives  82.3 us (6%)
  other arithmetic  66.6 us (5%)
  starting transfers between devices  32 us (2%)
  between operations  17.3 us (1%)
    ppermute x7, waiting for transfers between devices, per_device(): lax.ppermute(ring[-1], 'fsdp', [(dev, (dev + 1) % 8) for dev in range(8)])  201 us
    reduce_scatter x1, waiting for transfers between devices, per_device(): lax.psum_scatter(partial_back, 'fsdp', scatter_dimension=0, tiled=True)  195 us
    psum x1, waiting for transfers between devices, per_device(): lax.psum(shard_qkv.astype(jnp.bfloat16), 'seq').astype(jnp.float32)  156 us
    reduce_scatter x1, waiting for transfers between devices, per_device(): lax.psum_scatter(partial_out.astype(jnp.bfloat16), 'fsdp', scatter_dimens...  119 us
    reduce_scatter x1, waiting for transfers between devices, per_device(): lax.psum_scatter(term_qkv.astype(jnp.bfloat16), 'fsdp', scatter_dimension...  79.8 us
    unnamed x2, blocking collectives  59.2 us
    all_gather x1, waiting for transfers between devices, per_device(): lax.all_gather(qkv_weight, 'fsdp', axis=0, tiled=True)  52.2 us
    unnamed x116, local copies, waits for them, and re-layouts  44.3 us
  transfers between devices with their start and end apart: 23, of which 18 were waited for; matrix products, arithmetic and copies ran while one was open for 18% of the time, Pallas kernels for 0%

profile of v1, /device:TPU:0, one launch (start us, length us, event | category | flops | bytes accessed | tf_op | source)
XLA Modules:
  0.0 1335.7 jit_solution(9731253927210930281)
XLA Ops:
  12.4 23.9 %all-reduce.6 = (bf16[1536]{0:T(1024)(128)(2,1)S(1)}, bf16[1536]{0:T(1024)(128)(2,1)S(1)}) all-reduce(bf16[1536]{0:T(1024)(128)(2,1)S(1)} %dynamic-update-slice, bf16[1536]{0:T(1024)(128)(2,1)S(1)} %dynamic-update-slice.1), channel_id=1, replica_groups=mesh['seq'=4,'fsdp'=8] {'fsdp'}, use_global_device_ids=true, to_apply=%add | all-reduce | flops 3072 | bytes 12288
  38.4 16.5 %all-gather = bf16[8,1,256]{2,1,0:T(2,128)(2,1)S(1)} all-gather(bf16[1,1,256]{2,1,0:T(2,128)(2,1)S(1)} %reshape.304), channel_id=1, replica_groups=mesh['seq'=4,'fsdp'=8] {'fsdp'}, dimensions={0}, use_global_device_ids=true | all-gather | bytes 4608 | tf_op jit(solution)/shard_map/all_gather | solution.py:151
  60.3 52.2 %all-gather.5.cloned.1.call-done = bf16[1536,2048]{1,0:T(8,128)(2,1)} async-done(((bf16[192,2048]{1,0:T(8,128)(2,1)}), bf16[1536,2048]{1,0:T(8,128)(2,1)}) %all-gather.5.cloned.1.call-update) | async-done | bytes 6291472 | tf_op jit(solution)/shard_map/all_gather | solution.py:150
  112.5 4.9 convolution_add_fusion.2
  120.0 3.2 copy.120
  126.3 4.0 all-to-all-start.1
  136.4 4.2 all-to-all-start
  142.2 10.1 all-to-all-done
  154.0 4.5 all-to-all-start.2
  165.9 23.9 %while.27 = (s32[]{:T(128)}, bf16[2,512,3,128]{3,1,2,0:T(8,128)(2,1)}, f32[2,3,512]{2,1,0:T(4,128)S(1)}, s32[2]{0:T(128)S(1)}, bf16[1024,3,128]{2,0,1:T(8,128)(2...) while((s32[]{:T(128)}, ...), condition=%wide.region_4.5_spmd, body=%wide.region_1.4_spmd.sunk | while | flops 824900608 | bytes 22342304 | solution.py:79
  174.0 3.8 fusion.129
  185.9 3.8 fusion.129
  192.6 5.6 reshape.317
  198.7 7.3 reduce.2
  207.9 4.2 all-to-all-start.3
  212.4 11.5 all-to-all-done.3
  223.9 3.7 reshape.323
  232.3 4.3 multiply_reduce_fusion.2
  239.4 33.5 %collective-permute-done = bf16[256,1536]{1,0:T(8,128)(2,1)S(1)} collective-permute-done((bf16[256,1536]{1,0:T(8,128)(2,1)}, bf16[256,1536]{1,0:T(8,128)(2,1)S(1)}, u32[]{:S(2)}, u32[]{:S(2)}) %collective-permute-start) | collective-permute-done | bytes 786464 | tf_op jit(solution)/shard_map/ppermute | solution.py:205
  273.8 29.5 %collective-permute-done.1 = bf16[256,1536]{1,0:T(8,128)(2,1)S(1)} collective-permute-done((bf16[256,1536]{1,0:T(8,128)(2,1)S(1)}, bf16[256,1536]{1,0:T(8,128)(2,1)S(1)}, u32[]{:S(2)}, u32[]{:S(2)}) %collective-permute-start.1) | collective-permute-done | bytes 786464 | tf_op jit(solution)/shard_map/ppermute | solution.py:205
  304.2 39.0 %collective-permute-done.2 = bf16[256,1536]{1,0:T(8,128)(2,1)S(1)} collective-permute-done((bf16[256,1536]{1,0:T(8,128)(2,1)S(1)}, bf16[256,1536]{1,0:T(8,128)(2,1)S(1)}, u32[]{:S(2)}, u32[]{:S(2)}) %collective-permute-start.2) | collective-permute-done | bytes 786464 | tf_op jit(solution)/shard_map/ppermute | solution.py:205
  344.1 38.8 %collective-permute-done.3 = bf16[256,1536]{1,0:T(8,128)(2,1)S(1)} collective-permute-done((bf16[256,1536]{1,0:T(8,128)(2,1)S(1)}, bf16[256,1536]{1,0:T(8,128)(2,1)S(1)}, u32[]{:S(2)}, u32[]{:S(2)}) %collective-permute-start.3) | collective-permute-done | bytes 786464 | tf_op jit(solution)/shard_map/ppermute | solution.py:205
  383.8 20.9 %collective-permute-done.4 = bf16[256,1536]{1,0:T(8,128)(2,1)S(1)} collective-permute-done((bf16[256,1536]{1,0:T(8,128)(2,1)S(1)}, bf16[256,1536]{1,0:T(8,128)(2,1)S(1)}, u32[]{:S(2)}, u32[]{:S(2)}) %collective-permute-start.4) | collective-permute-done | bytes 786464 | tf_op jit(solution)/shard_map/ppermute | solution.py:205
  405.5 20.1 %collective-permute-done.5 = bf16[256,1536]{1,0:T(8,128)(2,1)} collective-permute-done((bf16[256,1536]{1,0:T(8,128)(2,1)S(1)}, bf16[256,1536]{1,0:T(8,128)(2,1)}, u32[]{:S(2)}, u32[]{:S(2)}) %collective-permute-start.5) | collective-permute-done | bytes 786464 | tf_op jit(solution)/shard_map/ppermute | solution.py:205
  425.6 19.3 %collective-permute-done.6 = bf16[256,1536]{1,0:T(8,128)(2,1)} collective-permute-done((bf16[256,1536]{1,0:T(8,128)(2,1)}, bf16[256,1536]{1,0:T(8,128)(2,1)}, u32[]{:S(2)}, u32[]{:S(2)}) %collective-permute-start.6) | collective-permute-done | bytes 786464 | tf_op jit(solution)/shard_map/ppermute | solution.py:205
  466.0 13.0 fusion.82
  479.0 9.6 fusion.83
  488.7 18.1 %multiply_convert_fusion = (bf16[2048,1120]{0,1:T(8,128)(2,1)}, bf16[2048,1120]{0,1:T(8,128)(2,1)}, bf16[2048,1120]{0,1:T(8,128)(2,1)}) fusion(f32[2048,1120]{0,1:T(8,128)} %fusion.82, f32[2048,1120]{0,1:T(8,128)} %fusion.83, bf16[1120,1536]{1,0:T(8,128)(2,1)S(1)} %copy-done, bf16[4096,1536]{1,0:T(8,128)(2,1)} %constant_dynamic-update-slice_fusion, ...), kind=kOutput, calls=%fused_computation.56 | convolution fusion | flops 7080837120 | bytes 41844740 | tf_op jit(solution)/shard_map/tm,fm->tf/dot_general | solution.py:209
  506.8 11.7 fusion.84
  518.5 13.9 %convolution_add_fusion = f32[2048,1536]{1,0:T(8,128)} fusion(f32[2048,1536]{1,0:T(8,128)S(1)} %fusion.84, bf16[2048,1120]{0,1:T(8,128)(2,1)} %get-tuple-element.263, bf16[1120,1536]{1,0:T(8,128)(2,1)S(1)} %copy-done.45), kind=kOutput, calls=%fused_computation.61 | convolution fusion | flops 7049576448 | bytes 33193984 | tf_op jit(solution)/shard_map/dot_general | solution.py:216
  532.5 12.4 convolution_convert_fusion
  545.0 195.3 %reduce-scatter.7.cloned.1.call-done = f32[256,1536]{1,0:T(8,128)} async-done(((f32[2048,1536]{1,0:T(8,128)}), f32[256,1536]{1,0:T(8,128)}) %reduce-scatter.7.cloned.1.call-update) | async-done | bytes 1572880 | tf_op jit(solution)/shard_map/reduce_scatter | solution.py:219
  742.8 118.7 %reduce-scatter.5.cloned.1.call-done = bf16[256,1536]{1,0:T(8,128)(2,1)} async-done(((bf16[2048,1536]{1,0:T(8,128)(2,1)}), bf16[256,1536]{1,0:T(8,128)(2,1)}) %reduce-scatter.5.cloned.1.call-update) | async-done | bytes 786448 | tf_op jit(solution)/shard_map/reduce_scatter | solution.py:200
  861.4 3.2 multiply_add_fusion
  864.7 4.3 convolution_convert_fusion.6
  870.2 3.5 all-to-all-start.4
  873.8 3.6 convolution_convert_fusion.5
  877.4 7.9 all-to-all-done.4
  886.5 47.3 %while.28 = (s32[]{:T(128)}, f32[1024,128]{1,0:T(8,128)}, f32[1024,128]{1,0:T(8,128)}, bf16[2,512,3,128]{3,1,2,0:T(8,128)(2,1)}, s32[2]{0:T(128)S(1)}, /*index=5...) while((s32[]{:T(128)}, f32[1024,128]{1,0:T(8,128)}, ...), condition=%wide.region_11.12_spmd.clone, body=%wide.region_9.11_spmd.clone.sunk | while | flops 2038234112 | bytes 90227544 | solution.py:120
  892.3 4.3 fusion.139
  901.3 2.9 fusion.141
  904.2 6.0 fusion.142
  915.8 4.3 fusion.139
  924.8 3.1 fusion.141
  927.8 6.0 fusion.142
  936.7 3.4 all-to-all-start.6
  941.7 4.4 all-to-all-done.6
  946.1 3.6 all-to-all-start.7
  952.4 5.5 reduce.5
  959.7 3.5 all-to-all-start.5
  965.2 9.7 all-to-all-done.5
  980.2 4.7 convolution_convert_fusion.1
  984.9 12.3 convolution_convert_fusion.2
  997.2 12.1 convolution_convert_fusion.3
  1009.3 12.0 convolution_convert_fusion.4
  1021.3 79.8 %reduce-scatter.9.cloned.1.call-done = bf16[192,2048]{1,0:T(8,128)(2,1)} async-done(((bf16[1536,2048]{1,0:T(8,128)(2,1)}), bf16[192,2048]{1,0:T(8,128)(2,1)}) %reduce-scatter.9.cloned.1.call-update) | async-done | bytes 786448 | tf_op jit(solution)/shard_map/reduce_scatter | solution.py:298
  1102.8 6.1 fusion.60
  1109.0 35.3 %all-reduce.5 = (bf16[1536]{0:T(1024)(128)(2,1)S(1)}, bf16[2048]{0:T(1024)(128)(2,1)S(1)}, bf16[1536]{0:T(1024)(128)(2,1)S(1)}) all-reduce(bf16[1536]{0:T(1024)(128)(2,1)S(1)} %get-tuple-element.210, bf16[2048]{0:T(1024)(128)(2,1)S(1)} %fusion.77, bf16[1536]{0:T(1024)(128)(2,1)S(1)} %copy-done.42), channel_id=4, replica_groups=mesh['seq'=4,'fsdp'=8] {'fsdp'}, use_global_device_ids=true, to_apply=%region_16.17.clone | all-reduce | flops 5120 | bytes 20480
  1144.5 6.5 all-reduce.7
  1152.8 3.0 fusion.59
  1155.7 156.5 %all-reduce.11.cloned.1.call-done = (bf16[192,2048]{1,0:T(8,128)(2,1)}, bf16[192,1536]{1,0:T(8,128)(2,1)}, bf16[1120,1536]{1,0:T(8,128)(2,1)}, bf16[1120,1536]{1,0:T(8,128)(2,1)}, bf16[1120,1536]{1,0:T(8,128)(2,1)}) async-done(((bf16[192,2048]{1,0:T(8,128)(2,1)}, bf16[192,1536]{1,0:T(8,128)(2,1)}, bf16[1120,1536]{1,0:T(8,128)(2,1)}, bf16[1120,1536]{1,0:T(8,128)(2,1)}, bf16[1120,1536]{1,0:T(8,128)(2,1)}), ...) | async-done | bytes 11698192 | tf_op jit(solution)/shard_map/psum | solution.py:313
  1312.2 6.0 convert_element_type.265
  1318.2 3.9 convert_element_type.267
  1322.1 3.8 convert_element_type.269
  (259 shorter events, 127.5 us)
Async XLA Ops:
  7.2 481.5 %copy-start = (bf16[1120,1536]{1,0:T(8,128)(2,1)S(1)}, bf16[1120,1536]{1,0:T(8,128)(2,1)}, u32[]{:S(2)}) copy-start(bf16[1120,1536]{1,0:T(8,128)(2,1)} %param.24) | copy-start | bytes 10321924
  7.2 105.3 %all-gather.5.cloned.1.call-start = ((), (), s32[]{:S(2)}) async-start(), calls=%async_computation.12 | async-start | bytes 7077888 | tf_op jit(solution)/shard_map/all_gather | solution.py:150
  7.9 224.3 %all-gather.7.cloned.1.call-start = ((), (), s32[]{:S(2)}) async-start(), calls=%async_computation.13 | async-start | bytes 5308416 | tf_op jit(solution)/shard_map/all_gather | solution.py:152
  36.4 81.1 %copy-start.38 = (f32[1536]{0:T(1024)}, f32[1536]{0:T(1024)S(1)}, u32[]{:S(2)}) copy-start(f32[1536]{0:T(1024)S(1)} %convert_element_type.218) | copy-start | bytes 18436
  37.8 79.7 %copy-start.40 = (f32[256]{0:T(256)}, f32[256]{0:T(256)S(1)}, u32[]{:S(2)}) copy-start(f32[256]{0:T(256)S(1)} %add_rsqrt_fusion.1) | copy-start | bytes 3076
  117.4 1.3 copy-start.27
  126.3 10.1 all-to-all-start.1
  130.3 2.7 copy-start.31
  130.3 2.8 copy-start.9
  136.4 15.9 %all-to-all-start = ((bf16[256,4,384]{0,2,1:T(8,128)(2,1)}), bf16[256,4,384]{0,2,1:T(8,128)(2,1)}, u32[]{:S(2)}, u32[]{:S(2)}) async-start(bf16[256,4,384]{0,2,1:T(8,128)(2,1)} %fusion.63), calls=%async_computation | async-start | bytes 1572864 | tf_op jit(solution)/shard_map/all_to_all | solution.py:173
  154.0 12.0 all-to-all-start.2
  189.8 18.1 %copy-start.36 = (f32[2,3,512]{2,1,0:T(4,128)}, f32[2,3,512]{2,1,0:T(4,128)S(1)}, u32[]{:S(2)}) copy-start(f32[2,3,512]{2,1,0:T(4,128)S(1)} %get-tuple-element.434) | copy-start | bytes 36868
  207.9 15.9 %all-to-all-start.3 = ((bf16[4,2,49152]{2,1,0:T(2,128)(2,1)}), bf16[4,2,49152]{2,1,0:T(2,128)(2,1)}, u32[]{:S(2)}, u32[]{:S(2)}) async-start(bf16[4,2,49152]{2,1,0:T(2,128)(2,1)} %reshape.322), calls=%async_computation.3 | async-start | bytes 1572864 | tf_op jit(solution)/shard_map/all_to_all | solution.py:181
  212.1 253.9 %all-gather.9.cloned.1.call-start = ((), (), s32[]{:S(2)}) async-start(), calls=%async_computation.14 | async-start | bytes 7077888 | tf_op jit(solution)/shard_map/all_gather | solution.py:193
  238.8 501.5 %reduce-scatter.7.cloned.1.call-start = ((), (), s32[]{:S(2)}) async-start(), calls=%async_computation.16 | async-start | bytes 14155776 | tf_op jit(solution)/shard_map/reduce_scatter | solution.py:219
  238.8 34.0 %collective-permute-start = (bf16[256,1536]{1,0:T(8,128)(2,1)}, bf16[256,1536]{1,0:T(8,128)(2,1)S(1)}, u32[]{:S(2)}, u32[]{:S(2)}) collective-permute-start(bf16[256,1536]{1,0:T(8,128)(2,1)} %bitcast.266), channel_id=1, source_target_pairs={{0,1},{1,2},{2,3},{3,4},{4,5},{5,6},{6,7},{7,0},{8,9},{9,10},{10,1... | collective-permute-start | bytes 2359304 | tf_op jit(solution)/shard_map/ppermute | solution.py:205
  273.8 29.5 %collective-permute-start.1 = (bf16[256,1536]{1,0:T(8,128)(2,1)S(1)}, bf16[256,1536]{1,0:T(8,128)(2,1)S(1)}, u32[]{:S(2)}, u32[]{:S(2)}) collective-permute-start(bf16[256,1536]{1,0:T(8,128)(2,1)S(1)} %collective-permute-done), channel_id=1, source_target_pairs={{0,1},{1,2},{2,3},{3,4},{4,5},{5,6},{6,7},{7,0},{8,9},{9,10},{10,1... | collective-permute-start | bytes 2359304 | tf_op jit(solution)/shard_map/ppermute | solution.py:205
  304.2 39.0 %collective-permute-start.2 = (bf16[256,1536]{1,0:T(8,128)(2,1)S(1)}, bf16[256,1536]{1,0:T(8,128)(2,1)S(1)}, u32[]{:S(2)}, u32[]{:S(2)}) collective-permute-start(bf16[256,1536]{1,0:T(8,128)(2,1)S(1)} %collective-permute-done.1), channel_id=1, source_target_pairs={{0,1},{1,2},{2,3},{3,4},{4,5},{5,6},{6,7},{7,0},{8,9},{9,10},{10,1... | collective-permute-start | bytes 2359304 | tf_op jit(solution)/shard_map/ppermute | solution.py:205
  344.1 38.8 %collective-permute-start.3 = (bf16[256,1536]{1,0:T(8,128)(2,1)S(1)}, bf16[256,1536]{1,0:T(8,128)(2,1)S(1)}, u32[]{:S(2)}, u32[]{:S(2)}) collective-permute-start(bf16[256,1536]{1,0:T(8,128)(2,1)S(1)} %collective-permute-done.2), channel_id=1, source_target_pairs={{0,1},{1,2},{2,3},{3,4},{4,5},{5,6},{6,7},{7,0},{8,9},{9,10},{10,1... | collective-permute-start | bytes 2359304 | tf_op jit(solution)/shard_map/ppermute | solution.py:205
  383.8 20.9 %collective-permute-start.4 = (bf16[256,1536]{1,0:T(8,128)(2,1)S(1)}, bf16[256,1536]{1,0:T(8,128)(2,1)S(1)}, u32[]{:S(2)}, u32[]{:S(2)}) collective-permute-start(bf16[256,1536]{1,0:T(8,128)(2,1)S(1)} %collective-permute-done.3), channel_id=1, source_target_pairs={{0,1},{1,2},{2,3},{3,4},{4,5},{5,6},{6,7},{7,0},{8,9},{9,10},{10,1... | collective-permute-start | bytes 2359304 | tf_op jit(solution)/shard_map/ppermute | solution.py:205
  405.5 20.1 %collective-permute-start.5 = (bf16[256,1536]{1,0:T(8,128)(2,1)S(1)}, bf16[256,1536]{1,0:T(8,128)(2,1)}, u32[]{:S(2)}, u32[]{:S(2)}) collective-permute-start(bf16[256,1536]{1,0:T(8,128)(2,1)S(1)} %collective-permute-done.4), channel_id=1, source_target_pairs={{0,1},{1,2},{2,3},{3,4},{4,5},{5,6},{6,7},{7,0},{8,9},{9,10},{10,1... | collective-permute-start | bytes 2359304 | tf_op jit(solution)/shard_map/ppermute | solution.py:205
  425.6 19.4 %collective-permute-start.6 = (bf16[256,1536]{1,0:T(8,128)(2,1)}, bf16[256,1536]{1,0:T(8,128)(2,1)}, u32[]{:S(2)}, u32[]{:S(2)}) collective-permute-start(bf16[256,1536]{1,0:T(8,128)(2,1)} %collective-permute-done.5), channel_id=1, source_target_pairs={{0,1},{1,2},{2,3},{3,4},{4,5},{5,6},{6,7},{7,0},{8,9},{9,10},{10,1... | collective-permute-start | bytes 2359304 | tf_op jit(solution)/shard_map/ppermute | solution.py:205
  425.6 25.7 %copy-start.24 = (bf16[256,1536]{1,0:T(8,128)(2,1)S(1)}, bf16[256,1536]{1,0:T(8,128)(2,1)}, u32[]{:S(2)}) copy-start(bf16[256,1536]{1,0:T(8,128)(2,1)} %copy-done.23) | copy-start | bytes 2359300
  425.6 26.6 %copy-start.22 = (bf16[256,1536]{1,0:T(8,128)(2,1)S(1)}, bf16[256,1536]{1,0:T(8,128)(2,1)}, u32[]{:S(2)}) copy-start(bf16[256,1536]{1,0:T(8,128)(2,1)} %copy-done.21) | copy-start | bytes 2359300
  425.6 27.6 %copy-start.20 = (bf16[256,1536]{1,0:T(8,128)(2,1)S(1)}, bf16[256,1536]{1,0:T(8,128)(2,1)}, u32[]{:S(2)}) copy-start(bf16[256,1536]{1,0:T(8,128)(2,1)} %copy-done.19) | copy-start | bytes 2359300
  425.6 28.5 %copy-start.18 = (bf16[256,1536]{1,0:T(8,128)(2,1)S(1)}, bf16[256,1536]{1,0:T(8,128)(2,1)}, u32[]{:S(2)}) copy-start(bf16[256,1536]{1,0:T(8,128)(2,1)} %copy-done.17) | copy-start | bytes 2359300
  447.0 8.0 copy-start.14
  452.2 7.9 copy-start.26
  466.0 13.0 copy-start.43
  466.0 13.0 copy-start.44
  506.8 11.7 copy-start.45
  532.5 329.0 %reduce-scatter.5.cloned.1.call-start = ((), (), s32[]{:S(2)}) async-start(), calls=%async_computation.15 | async-start | bytes 7077888 | tf_op jit(solution)/shard_map/reduce_scatter | solution.py:200
  544.9 195.4 %copy-start.6 = (f32[256,1536]{1,0:T(8,128)S(1)}, f32[256,1536]{1,0:T(8,128)}, u32[]{:S(2)}) copy-start(f32[256,1536]{1,0:T(8,128)} %copy-done.5) | copy-start | bytes 4718596
  864.7 9.1 copy-start.10
  864.7 9.1 copy-start.7
  870.2 15.1 %all-to-all-start.4 = ((bf16[256,4,384]{0,2,1:T(8,128)(2,1)}), bf16[256,4,384]{0,2,1:T(8,128)(2,1)S(1)}, u32[]{:S(2)}, u32[]{:S(2)}) async-start(bf16[256,4,384]{0,2,1:T(8,128)(2,1)} %bitcast.270), calls=%async_computation.6 | async-start | bytes 1572864 | tf_op jit(solution)/shard_map/all_to_all | solution.py:231
  873.7 147.6 %reduce-scatter.11.cloned.1.call-start = ((), (), s32[]{:S(2)}) async-start(), calls=%async_computation.18 | async-start | bytes 5308416 | tf_op jit(solution)/shard_map/reduce_scatter | solution.py:304
  877.4 9.1 copy-start.37
  886.7 10.0 copy-start.12
  891.3 5.3 copy-start.2
  892.3 4.3 copy-start.3
  901.3 2.9 copy-start.4
  904.2 6.0 copy-start.13
  910.2 10.0 copy-start.12
  914.8 5.3 copy-start.2
  915.8 4.3 copy-start.3
  924.8 3.1 copy-start.4
  927.8 6.0 copy-start.13
  936.7 9.4 all-to-all-start.6
  946.1 13.6 %all-to-all-start.7 = ((bf16[4,2,16384]{2,1,0:T(2,128)(2,1)}), bf16[4,2,16384]{2,1,0:T(2,128)(2,1)S(1)}, u32[]{:S(2)}, u32[]{:S(2)}) async-start(bf16[4,2,16384]{2,1,0:T(2,128)(2,1)} %reshape.324), calls=%async_computation.9 | async-start | bytes 524288 | tf_op jit(solution)/shard_map/all_to_all | solution.py:260
  952.4 11.0 copy-start.28
  952.4 11.1 copy-start.29
  959.7 3.8 copy-start.33
  959.7 15.1 %all-to-all-start.5 = ((bf16[4,2,49152]{2,1,0:T(2,128)(2,1)}), bf16[4,2,49152]{2,1,0:T(2,128)(2,1)S(1)}, u32[]{:S(2)}, u32[]{:S(2)}) async-start(bf16[4,2,49152]{2,1,0:T(2,128)(2,1)} %reshape.328), calls=%async_computation.7 | async-start | bytes 1572864 | tf_op jit(solution)/shard_map/all_to_all | solution.py:246
  963.3 137.9 %reduce-scatter.9.cloned.1.call-start = ((), (), s32[]{:S(2)}) async-start(), calls=%async_computation.17 | async-start | bytes 7077888 | tf_op jit(solution)/shard_map/reduce_scatter | solution.py:298
  965.2 13.7 %copy-start.30 = (f32[256,128]{0,1:T(8,128)S(1)}, f32[256,128]{0,1:T(8,128)}, u32[]{:S(2)}) copy-start(f32[256,128]{0,1:T(8,128)} %copy.95) | copy-start | bytes 393220
  984.9 327.3 %all-reduce.11.cloned.1.call-start = ((), (), s32[]{:S(2)}) async-start(), calls=%async_computation.19 | async-start | bytes 23396352 | tf_op jit(solution)/shard_map/psum | solution.py:313
  1102.8 6.1 copy-start.42
  1102.8 49.9 %copy-start.11 = (f32[256,1536]{1,0:T(8,128)S(1)}, f32[256,1536]{1,0:T(8,128)}, u32[]{:S(2)}) copy-start(f32[256,1536]{1,0:T(8,128)} %copy-done.10) | copy-start | bytes 4718596
  1312.2 6.0 copy-start.16
  1318.2 3.9 copy-start.15
  1322.1 3.9 copy-start.34
  1322.1 5.2 copy-start.35
  1322.1 6.3 copy-start.1
  (10 other events, 9.9 us)
Sparse Core Ops, SparseCore 0:
  10.2 102.2 all-gather.4
  114.7 78.0 all-gather.6
  238.9 140.2 all-gather.8
  532.6 207.6 reduce-scatter.6
  744.3 117.0 reduce-scatter.4
  878.4 94.8 reduce-scatter.10
  985.0 116.1 reduce-scatter.8
  1104.7 207.4 all-reduce.10
